TPU v7x, 512 devices: a whole 4x4x16 slice. The times are simulated.
512 devices in a mesh: row: 32 (over z_lo, y), col: 16 (over z_hi, x, core).
Axes of the slice: x: 4, y: 4, z: 16 (z_hi: 2, z_lo: 8; z = z_hi * 8 + z_lo), core: 2. Of those that a mesh axis runs over, the one named last changes fastest.
Arguments:
- prefill_hidden: bfloat16 [4, 2048, 2880], P(None, 'row', 'col'), may hold values from -6 to 6
- decode_hidden: bfloat16 [128, 2880], P('row', 'col'), may hold values from -6 to 6
- norm_gain: bfloat16 [2880], replicated, may hold values from 0.5 to 1.5
- query_weight: bfloat16 [2880, 4096], P('row', 'col'), may hold values from -0.11388673 to 0.11388673
- kv_weight: bfloat16 [2880, 2, 512], P('row'), may hold values from -0.11388673 to 0.11388673
- out_weight: bfloat16 [4096, 2880], P('col', 'row'), may hold values from -0.09375 to 0.09375
- sink_logits: bfloat16 [64], P('col'), may hold values from -4 to 4
- key_pool: bfloat16 [768, 64, 512], P('row'), may hold values from -6 to 6
- value_pool: bfloat16 [768, 64, 512], P('row'), may hold values from -6 to 6
- lengths: int32 [32, 4], P('row'), may hold values from 1 to 384, 960 in all within a row
- page_table: int32 [32, 24], P('row'), may hold values from 0 to 23, each once within a row
Outputs:
- prefill_out: bfloat16 [4, 2048, 2880], P(None, 'row', 'col')
- decode_out: bfloat16 [128, 2880], P('row', 'col')
Inputs may be any that keep to these rules, and one draw needn't show every extreme that they name: The 4 cached lengths of one index of row sum to 960, and some request has length 384. `page_table`: each line lists every local page of one index of row exactly once; request r % 4 of that index owns entries (r % 4) * 6 to (r % 4 + 1) * 6 - 1.
All inputs are finite; a program needn't handle non-finite values.
Results may differ from a plain program's by a relative error of at most 0.012.
Values may be sent and summed in bfloat16 or wider, within the bound.
A program may use at most 64 MiB of HBM per device.

v0:
```python
import math
import jax
import jax.numpy as jnp
from jax import lax
from jax.sharding import PartitionSpec as P

HQ = 64
KV = 8
HD = 64


def normed(token_rows, norm_gain):
    widened = token_rows.astype(jnp.float32)
    inverse = lax.rsqrt(jnp.mean(widened * widened, axis=-1, keepdims=True) + 1e-05)
    return (widened * inverse * norm_gain.astype(jnp.float32)).astype(jnp.bfloat16)


def body(
    prefill_hidden,
    decode_hidden,
    norm_gain,
    query_weight,
    kv_weight,
    out_weight,
    sink_logits,
    key_pool,
    value_pool,
    lengths,
    page_table,
):
    spans, span_rows, col_width = prefill_hidden.shape
    decode_rows = decode_hidden.shape[0]
    prefill_count = spans * span_rows
    token_rows = jnp.concatenate(
        [prefill_hidden.reshape(prefill_count, col_width), decode_hidden], axis=0
    )
    features = lax.all_gather(token_rows, "col", axis=1, tiled=True)
    hidden = normed(features, norm_gain)
    heads_dev = query_weight.shape[1] // HD
    group_size = HQ // KV
    kv_dev = max(1, heads_dev // group_size)
    per_kv = heads_dev // kv_dev
    col_index = lax.axis_index("col")
    row_index = lax.axis_index("row")
    kv_first = col_index * heads_dev // group_size
    kv_columns = lax.dynamic_slice_in_dim(kv_weight, kv_first * HD, kv_dev * HD, 2).reshape(
        kv_weight.shape[0], 2 * kv_dev * HD
    )
    query_full, kv_full = (
        lax.all_gather(query_weight, "row", axis=0, tiled=True),
        lax.all_gather(kv_columns, "row", axis=0, tiled=True),
    )
    query_sum = jnp.dot(hidden, query_full, preferred_element_type=jnp.float32)
    kv_sum = jnp.dot(hidden, kv_full, preferred_element_type=jnp.float32)
    queries = query_sum.astype(jnp.bfloat16)
    key_rows = kv_sum[:, : kv_dev * HD].astype(jnp.bfloat16)
    value_rows = kv_sum[:, kv_dev * HD :].astype(jnp.bfloat16)
    score_scale = 1.0 / math.sqrt(HD)
    sink_grid = sink_logits.astype(jnp.float32).reshape(kv_dev, per_kv)
    query_pre = queries[:prefill_count].reshape(spans, span_rows, kv_dev, per_kv, HD)
    key_pre = key_rows[:prefill_count].reshape(spans, span_rows, kv_dev * HD)
    value_pre = value_rows[:prefill_count].reshape(spans, span_rows, kv_dev * HD)
    positions = row_index * span_rows + jnp.arange(span_rows, dtype=jnp.int32)
    state_shape = (spans, kv_dev, per_kv, span_rows)
    pieces = (
        lax.all_gather(key_pre, "row", axis=1, tiled=True),
        lax.all_gather(value_pre, "row", axis=1, tiled=True),
    )
    running = jnp.broadcast_to(sink_grid[None, :, :, None], state_shape)
    denominator = jnp.ones(state_shape, jnp.float32)
    weighted = jnp.zeros(state_shape + (HD,), jnp.float32)
    piece_len = pieces[0].shape[1]
    key_piece = pieces[0].reshape(spans, piece_len, kv_dev, HD)
    value_piece = pieces[1].reshape(spans, piece_len, kv_dev, HD)
    scores = (
        jnp.einsum("nqkgd,npkd->nkgqp", query_pre, key_piece, preferred_element_type=jnp.float32)
        * score_scale
    )
    key_pos = jnp.arange(piece_len, dtype=jnp.int32)
    allowed = key_pos[None, :] <= positions[:, None]
    scores = jnp.where(allowed, scores, -jnp.inf)
    newest = jnp.maximum(running, jnp.max(scores, axis=-1))
    probs_soft = jnp.exp(scores - newest[..., None])
    factor = jnp.exp(running - newest)
    denominator = denominator * factor + jnp.sum(probs_soft, axis=-1)
    weighted = weighted * factor[..., None] + jnp.einsum(
        "nkgqp,npkd->nkgqd",
        probs_soft.astype(jnp.bfloat16),
        value_piece,
        preferred_element_type=jnp.float32,
    )
    running, denominator, weighted = (newest, denominator, weighted)
    prefill_att = (
        (weighted / denominator[..., None])
        .transpose(0, 3, 1, 2, 4)
        .reshape(prefill_count, heads_dev * HD)
        .astype(jnp.bfloat16)
    )
    query_dec = queries[prefill_count:].reshape(decode_rows, kv_dev, per_kv, HD)
    key_new = key_rows[prefill_count:].reshape(decode_rows, kv_dev, HD)
    value_new = value_rows[prefill_count:].reshape(decode_rows, kv_dev, HD)
    pool_pages, page_len, pool_width = key_pool.shape
    table = page_table.reshape(decode_rows, -1)
    max_pages = table.shape[1]
    key_mine = lax.dynamic_slice_in_dim(
        key_pool.reshape(pool_pages, page_len, KV, HD), kv_first, kv_dev, 2
    )
    value_mine = lax.dynamic_slice_in_dim(
        value_pool.reshape(pool_pages, page_len, KV, HD), kv_first, kv_dev, 2
    )
    key_cache = key_mine[table].reshape(decode_rows, max_pages * page_len, kv_dev, HD)
    value_cache = value_mine[table].reshape(decode_rows, max_pages * page_len, kv_dev, HD)
    cache_scores = (
        jnp.einsum("skgd,stkd->skgt", query_dec, key_cache, preferred_element_type=jnp.float32)
        * score_scale
    )
    live = (
        jnp.arange(max_pages * page_len, dtype=jnp.int32)[None, :]
        < lengths.reshape(decode_rows)[:, None]
    )
    cache_scores = jnp.where(live[:, None, None, :], cache_scores, -jnp.inf)
    self_scores = (
        jnp.einsum("skgd,skd->skg", query_dec, key_new, preferred_element_type=jnp.float32)
        * score_scale
    )
    highest = jnp.maximum(jnp.maximum(jnp.max(cache_scores, axis=-1), self_scores), sink_grid[None])
    cache_probs = jnp.exp(cache_scores - highest[..., None])
    self_probs = jnp.exp(self_scores - highest)
    denom_dec = jnp.sum(cache_probs, axis=-1) + self_probs + jnp.exp(sink_grid[None] - highest)
    decode_sum = jnp.einsum(
        "skgt,stkd->skgd",
        cache_probs.astype(jnp.bfloat16),
        value_cache,
        preferred_element_type=jnp.float32,
    )
    decode_sum = (
        decode_sum
        + self_probs.astype(jnp.bfloat16).astype(jnp.float32)[..., None]
        * value_new.astype(jnp.float32)[:, :, None, :]
    )
    decode_att = (
        (decode_sum / denom_dec[..., None])
        .reshape(decode_rows, heads_dev * HD)
        .astype(jnp.bfloat16)
    )
    attended = jnp.concatenate([prefill_att, decode_att], axis=0)
    partial_out = jnp.dot(
        attended,
        lax.all_gather(out_weight, "row", axis=1, tiled=True),
        preferred_element_type=jnp.float32,
    )
    summed = lax.psum_scatter(
        partial_out.astype(jnp.bfloat16), "col", scatter_dimension=1, tiled=True
    ).astype(jnp.float32)
    result = (token_rows.astype(jnp.float32) + summed).astype(jnp.bfloat16)
    return (result[:prefill_count].reshape(spans, span_rows, col_width), result[prefill_count:])


def solution(mesh):
    in_specs = (
        P(None, "row", "col"),
        P("row", "col"),
        P(),
        P("row", "col"),
        P("row", None, None),
        P("col", "row"),
        P("col"),
        P("row", None, None),
        P("row", None, None),
        P("row", None),
        P("row", None),
    )
    out_specs = (P(None, "row", "col"), P("row", "col"))
    return jax.shard_map(body, mesh=mesh, in_specs=in_specs, out_specs=out_specs, check_vma=False)
```

profile of v0, /device:TPU:1, one launch (start us, length us, event | category | flops | bytes accessed | tf_op | source)
XLA Modules:
  0.0 1276.0 jit_solution(622490899157801376)
XLA Ops:
  7.2 1.6 fusion.37
  10.8 126.2 %all-gather.1 = bf16[32,90,128]{2,1,0:T(8,128)(2,1)S(1)} all-gather(bf16[1,90,128]{2,1,0:T(8,128)(2,1)S(1)} %copy.43), channel_id=1, replica_groups=mesh['row'=32,'col'=16] {'row'}, dimensions={0}, use_global_device_ids=true | all-gather | bytes 760320 | tf_op jit(solution)/shard_map/all_gather | solution.py:51
  138.1 4.2 copy_convert_fusion
  142.3 4.4 reshape.272
  149.4 5.1 reshape.231
  154.5 5.2 reshape.234
  159.7 5.5 constant_dynamic-slice_fusion
  167.3 2.0 copy.71
  169.3 2.4 gather_fusion
  171.7 2.4 gather_fusion.1
  174.6 128.9 %all-gather.16.cloned.1.call-done = bf16[32,90,256]{2,1,0:T(8,128)(2,1)} async-done(((bf16[1,90,256]{2,1,0:T(8,128)(2,1)}), bf16[32,90,256]{2,1,0:T(8,128)(2,1)}) %all-gather.16.cloned.1.call-update) | async-done | bytes 1474576 | tf_op jit(solution)/shard_map/all_gather | solution.py:50
  303.5 3.4 reshape.268
  306.9 2.1 convolution_convert_fusion.1
  309.4 1.3 fusion.52
  312.2 214.0 %all-gather.18.cloned.1.call-done = bf16[32,90,256]{2,1,0:T(8,128)(2,1)} async-done(((bf16[1,90,256]{2,1,0:T(8,128)(2,1)}), bf16[32,90,256]{2,1,0:T(8,128)(2,1)}) %all-gather.18.cloned.1.call-update) | async-done | bytes 1474576 | tf_op jit(solution)/shard_map/all_gather | solution.py:149
  526.2 2.3 reshape.270
  528.6 221.9 %all-gather.10.cloned.1.call-done = bf16[4,2048,64]{2,1,0:T(8,128)(2,1)} async-done(((bf16[4,64,64]{2,1,0:T(8,128)(2,1)}), bf16[4,2048,64]{2,1,0:T(8,128)(2,1)}) %all-gather.10.cloned.1.call-update) | async-done | bytes 1048592 | tf_op jit(solution)/shard_map/all_gather | solution.py:66
  750.5 3.1 fusion.2
  753.7 2.2 fusion
  756.9 217.0 %all-gather.12.cloned.1.call-done = bf16[4,2048,64]{2,1,0:T(8,128)(2,1)} async-done(((bf16[4,64,64]{2,1,0:T(8,128)(2,1)}), bf16[4,2048,64]{2,1,0:T(8,128)(2,1)}) %all-gather.12.cloned.1.call-update) | async-done | bytes 1048592 | tf_op jit(solution)/shard_map/all_gather | solution.py:67
  973.9 6.2 fusion.28
  980.5 1.8 convolution_convert_fusion
  982.3 1.3 dynamic-slice
  984.2 282.6 %all-reduce.3.cloned.1.call-done = bf16[260,2880]{1,0:T(8,128)(2,1)} async-done(((bf16[260,2880]{1,0:T(8,128)(2,1)}), bf16[260,2880]{1,0:T(8,128)(2,1)}) %all-reduce.3.cloned.1.call-update) | async-done | bytes 1497616
  (69 shorter events, 14.1 us)
Async XLA Ops:
  7.2 3.3 copy-start
  7.2 130.9 %copy-start.5 = (bf16[2880]{0:T(1024)(128)(2,1)S(1)}, bf16[2880]{0:T(1024)(128)(2,1)}, u32[]{:S(2)}) copy-start(bf16[2880]{0:T(1024)(128)(2,1)} %param.13) | copy-start | bytes 17284
  7.2 130.9 %all-gather.14.cloned.1.call-start = ((), (), s32[]{:S(2)}) async-start(), calls=%async_computation.2 | async-start | bytes 2297856 | tf_op jit(solution)/shard_map/all_gather | solution.py:37
  8.9 294.6 %all-gather.16.cloned.1.call-start = ((), (), s32[]{:S(2)}) async-start(), calls=%async_computation.3 | async-start | bytes 1622016 | tf_op jit(solution)/shard_map/all_gather | solution.py:50
  9.6 516.6 %all-gather.18.cloned.1.call-start = ((), (), s32[]{:S(2)}) async-start(), calls=%async_computation.4 | async-start | bytes 1622016 | tf_op jit(solution)/shard_map/all_gather | solution.py:149
  10.4 740.1 %all-gather.10.cloned.1.call-start = ((), (), s32[]{:S(2)}) async-start(), calls=%async_computation | async-start | bytes 2162688 | tf_op jit(solution)/shard_map/all_gather | solution.py:66
  146.7 1.1 copy-start.2
  146.7 2.6 copy-start.7
  149.3 824.6 %all-gather.12.cloned.1.call-start = ((), (), s32[]{:S(2)}) async-start(), calls=%async_computation.1 | async-start | bytes 2162688 | tf_op jit(solution)/shard_map/all_gather | solution.py:67
  159.7 6.8 copy-start.8
  159.7 14.4 %copy-start.6 = (s32[1,4]{1,0:T(1,128)S(1)}, s32[1,4]{1,0:T(1,128)}, u32[]{:S(2)}) copy-start(s32[1,4]{1,0:T(1,128)} %param.20) | copy-start | bytes 52
  174.3 1092.5 %all-reduce.3.cloned.1.call-start = ((), (), s32[]{:S(2)}) async-start(), calls=%async_computation.5 | async-start | bytes 3108864
  753.6 3.2 copy-start.1
  980.5 286.4 %copy-start.3 = (bf16[4,64,180]{2,1,0:T(8,128)(2,1)S(1)}, bf16[4,64,180]{2,1,0:T(8,128)(2,1)}, u32[]{:S(2)}) copy-start(bf16[4,64,180]{2,1,0:T(8,128)(2,1)} %param.11) | copy-start | bytes 276484
  980.5 286.4 %copy-start.4 = (bf16[4,180]{1,0:T(4,128)(2,1)S(1)}, bf16[4,180]{1,0:T(4,128)(2,1)}, u32[]{:S(2)}) copy-start(bf16[4,180]{1,0:T(4,128)(2,1)} %param.12) | copy-start | bytes 4324
Sparse Core Ops, SparseCore 0:
  11.2 99.8 all-gather.13
  113.1 190.3 all-gather.15
  305.6 220.6 all-gather.17
  528.8 221.7 all-gather.9
  752.4 221.4 all-gather.11
  982.4 284.3 all-reduce.2
where the time goes:
time: 1280 us
  waiting for transfers between devices  1070 us (84%)
  blocking collectives  126 us (10%)
  local copies, waits for them, and re-layouts  41.3 us (3%)
  matrix products  16.5 us (1%)
  between operations  15 us (1%)
    unnamed x7, waiting for transfers between devices  284 us
    all_gather x1, waiting for transfers between devices, body(): lax.all_gather(key_pre, 'row', axis=1, tiled=True)  222 us
    all_gather x1, waiting for transfers between devices, body(): lax.all_gather(value_pre, 'row', axis=1, tiled=True)  217 us
    all_gather x1, waiting for transfers between devices, body(): lax.all_gather(out_weight, 'row', axis=1, tiled=True)  214 us
    all_gather x1, waiting for transfers between devices, body(): lax.all_gather(query_weight, 'row', axis=0, tiled=True)  129 us
    all_gather x1, blocking collectives, body(): lax.all_gather(kv_columns, 'row', axis=0, tiled=True)  126 us
  transfers between devices with their start and end apart: 6, of which 5 were waited for; matrix products, arithmetic and copies ran while one was open for 4% of the time, Pallas kernels for 0%

commit v1 on v0

--- a/solution.py
+++ b/solution.py
@@ -3,6 +3,7 @@
 import jax.numpy as jnp
 from jax import lax
 from jax.sharding import PartitionSpec as P
+from jax.lax import all_to_all, axis_size
 
 HQ = 64
 KV = 8
@@ -46,8 +47,14 @@
     kv_columns = lax.dynamic_slice_in_dim(kv_weight, kv_first * HD, kv_dev * HD, 2).reshape(
         kv_weight.shape[0], 2 * kv_dev * HD
     )
+
+    def rest_the_sides(obj):
+        return jnp.concatenate(
+            all_to_all(jnp.stack([obj] * axis_size("row"), axis=0), "row", 0, 0), axis=0
+        )
+
     query_full, kv_full = (
-        lax.all_gather(query_weight, "row", axis=0, tiled=True),
+        rest_the_sides(query_weight),
         lax.all_gather(kv_columns, "row", axis=0, tiled=True),
     )
     query_sum = jnp.dot(hidden, query_full, preferred_element_type=jnp.float32)

time: 1280 us -> 1080 us (0.84)
  waiting for transfers between devices: 1070 us -> 838 us
  blocking collectives: 126 us -> 143 us
  starting transfers between devices: 0.42 us -> 16.7 us
    all_gather x1 -> x0, waiting for transfers between devices: 129 us -> none  [body(): lax.all_gather(query_weight, 'row', axis=0, tiled=True)]
    all_gather x1, waiting for transfers between devices: 214 us -> 123 us  [body(): lax.all_gather(out_weight, 'row', axis=1, tiled=True)]
    all_gather x1, blocking collectives: 126 us -> 143 us  [body(): lax.all_gather(kv_columns, 'row', axis=0, tiled=True)]
    all_to_all x0 -> x1, starting transfers between devices: none -> 16.3 us  [rest_the_sides(): all_to_all(jnp.stack([obj] * axis_size('row'), axis=0), 'row', 0, 0)]
    unnamed x7 -> x6, waiting for transfers between devices: 284 us -> 283 us
  transfers between devices with their start and end apart: 6 -> 6, of which waited for: 5 -> 4; matrix products, arithmetic and copies ran while one was open for 4% -> 5% of each run, Pallas kernels for 0% -> 0%
where the time goes in v1:
time: 1080 us
  waiting for transfers between devices  838 us (78%)
  blocking collectives  143 us (13%)
  local copies, waits for them, and re-layouts  45.1 us (4%)
  starting transfers between devices  16.7 us (2%)
  between operations  14.7 us (1%)
  matrix products  14.6 us (1%)
    unnamed x6, waiting for transfers between devices  283 us
    all_gather x1, waiting for transfers between devices, body(): lax.all_gather(value_pre, 'row', axis=1, tiled=True)  217 us
    all_gather x1, waiting for transfers between devices, body(): lax.all_gather(key_pre, 'row', axis=1, tiled=True)  215 us
    all_gather x1, blocking collectives, body(): lax.all_gather(kv_columns, 'row', axis=0, tiled=True)  143 us
    all_gather x1, waiting for transfers between devices, body(): lax.all_gather(out_weight, 'row', axis=1, tiled=True)  123 us
  transfers between devices with their start and end apart: 6, of which 4 were waited for; matrix products, arithmetic and copies ran while one was open for 5% of the time, Pallas kernels for 0%

profile of v1, /device:TPU:1, one launch (start us, length us, event | category | flops | bytes accessed | tf_op | source)
XLA Modules:
  0.0 1082.2 jit_solution(12201793037360066054)
XLA Ops:
  7.2 1.6 fusion.37
  8.9 2.2 stack.2
  11.1 16.3 %all-to-all-start = ((bf16[32,90,256]{2,1,0:T(8,128)(2,1)}), bf16[32,90,256]{2,1,0:T(8,128)(2,1)}, u32[]{:S(2)}, u32[]{:S(2)}) async-start(bf16[32,90,256]{2,1,0:T(8,128)(2,1)} %stack.2), calls=%async_computation | async-start | bytes 3145728 | tf_op jit(solution)/shard_map/all_to_all | solution.py:53
  28.6 142.7 %all-gather.1 = bf16[32,90,128]{2,1,0:T(8,128)(2,1)S(1)} all-gather(bf16[1,90,128]{2,1,0:T(8,128)(2,1)S(1)} %copy.43), channel_id=1, replica_groups=mesh['row'=32,'col'=16] {'row'}, dimensions={0}, use_global_device_ids=true | all-gather | bytes 760320 | tf_op jit(solution)/shard_map/all_gather | solution.py:58
  172.4 4.2 copy_convert_fusion
  176.6 4.4 reshape.276
  183.7 5.2 reshape.237
  188.8 5.1 reshape.240
  194.0 5.5 constant_dynamic-slice_fusion
  201.6 1.9 copy.71
  203.6 2.4 gather_fusion
  205.9 2.3 gather_fusion.1
  208.8 122.6 %all-gather.14.cloned.1.call-done = bf16[32,90,256]{2,1,0:T(8,128)(2,1)} async-done(((bf16[1,90,256]{2,1,0:T(8,128)(2,1)}), bf16[32,90,256]{2,1,0:T(8,128)(2,1)}) %all-gather.14.cloned.1.call-update) | async-done | bytes 1474576 | tf_op jit(solution)/shard_map/all_gather | solution.py:156
  331.4 3.4 reshape.274
  334.8 3.4 reshape.232
  338.2 2.1 convolution_convert_fusion.1
  341.1 214.7 %all-gather.8.cloned.1.call-done = bf16[4,2048,64]{2,1,0:T(8,128)(2,1)} async-done(((bf16[4,64,64]{2,1,0:T(8,128)(2,1)}), bf16[4,2048,64]{2,1,0:T(8,128)(2,1)}) %all-gather.8.cloned.1.call-update) | async-done | bytes 1048592 | tf_op jit(solution)/shard_map/all_gather | solution.py:73
  555.8 3.1 fusion.2
  558.9 2.2 fusion
  562.2 217.0 %all-gather.10.cloned.1.call-done = bf16[4,2048,64]{2,1,0:T(8,128)(2,1)} async-done(((bf16[4,64,64]{2,1,0:T(8,128)(2,1)}), bf16[4,2048,64]{2,1,0:T(8,128)(2,1)}) %all-gather.10.cloned.1.call-update) | async-done | bytes 1048592 | tf_op jit(solution)/shard_map/all_gather | solution.py:74
  779.2 6.3 fusion.28
  787.1 1.8 convolution_convert_fusion
  788.9 1.3 dynamic-slice
  790.8 282.6 %all-reduce.3.cloned.1.call-done = bf16[260,2880]{1,0:T(8,128)(2,1)} async-done(((bf16[260,2880]{1,0:T(8,128)(2,1)}), bf16[260,2880]{1,0:T(8,128)(2,1)}) %all-reduce.3.cloned.1.call-update) | async-done | bytes 1497616
  (78 shorter events, 13.3 us)
Async XLA Ops:
  7.2 21.1 %copy-start = (bf16[90,2,512]{2,1,0:T(2,128)(2,1)S(1)}, bf16[90,2,512]{2,1,0:T(2,128)(2,1)}, u32[]{:S(2)}) copy-start(bf16[90,2,512]{2,1,0:T(2,128)(2,1)} %param.15) | copy-start | bytes 552964
  7.2 165.3 %all-gather.12.cloned.1.call-start = ((), (), s32[]{:S(2)}) async-start(), calls=%async_computation.3 | async-start | bytes 2297856 | tf_op jit(solution)/shard_map/all_gather | solution.py:38
  11.1 161.3 %copy-start.9 = (bf16[2880]{0:T(1024)(128)(2,1)S(1)}, bf16[2880]{0:T(1024)(128)(2,1)}, u32[]{:S(2)}) copy-start(bf16[2880]{0:T(1024)(128)(2,1)} %param.13) | copy-start | bytes 17284
  11.1 323.7 %all-to-all-start = ((bf16[32,90,256]{2,1,0:T(8,128)(2,1)}), bf16[32,90,256]{2,1,0:T(8,128)(2,1)}, u32[]{:S(2)}, u32[]{:S(2)}) async-start(bf16[32,90,256]{2,1,0:T(8,128)(2,1)} %stack.2), calls=%async_computation | async-start | bytes 3145728 | tf_op jit(solution)/shard_map/all_to_all | solution.py:53
  27.4 304.0 %all-gather.14.cloned.1.call-start = ((), (), s32[]{:S(2)}) async-start(), calls=%async_computation.4 | async-start | bytes 1622016 | tf_op jit(solution)/shard_map/all_gather | solution.py:156
  28.2 527.6 %all-gather.8.cloned.1.call-start = ((), (), s32[]{:S(2)}) async-start(), calls=%async_computation.1 | async-start | bytes 2162688 | tf_op jit(solution)/shard_map/all_gather | solution.py:73
  181.0 1.1 copy-start.3
  181.0 2.6 copy-start.11
  183.6 595.6 %all-gather.10.cloned.1.call-start = ((), (), s32[]{:S(2)}) async-start(), calls=%async_computation.2 | async-start | bytes 2162688 | tf_op jit(solution)/shard_map/all_gather | solution.py:74
  194.0 6.8 copy-start.12
  194.0 14.3 %copy-start.10 = (s32[1,4]{1,0:T(1,128)S(1)}, s32[1,4]{1,0:T(1,128)}, u32[]{:S(2)}) copy-start(s32[1,4]{1,0:T(1,128)} %param.20) | copy-start | bytes 52
  208.5 864.9 %all-reduce.3.cloned.1.call-start = ((), (), s32[]{:S(2)}) async-start(), calls=%async_computation.5 | async-start | bytes 3108864
  340.3 0.7 copy-start.5
  558.9 3.2 copy-start.1
  779.2 6.8 slice-start
  779.2 7.0 copy-start.4
  779.2 7.5 copy-start.7
  779.2 7.9 copy-start.2
  787.0 286.5 %copy-start.6 = (bf16[4,64,180]{2,1,0:T(8,128)(2,1)S(1)}, bf16[4,64,180]{2,1,0:T(8,128)(2,1)}, u32[]{:S(2)}) copy-start(bf16[4,64,180]{2,1,0:T(8,128)(2,1)} %param.11) | copy-start | bytes 276484
  787.0 286.4 %copy-start.8 = (bf16[4,180]{1,0:T(4,128)(2,1)S(1)}, bf16[4,180]{1,0:T(4,128)(2,1)}, u32[]{:S(2)}) copy-start(bf16[4,180]{1,0:T(4,128)(2,1)} %param.12) | copy-start | bytes 4324
Sparse Core Ops, SparseCore 0:
  11.2 103.4 all-gather.11
  116.8 214.5 all-gather.13
  334.1 221.6 all-gather.7
  557.7 221.4 all-gather.9
  789.0 284.3 all-reduce.2
